TPU v7x, 256 devices: a whole 4x4x8 slice. The times are simulated.
256 devices in a mesh: seq: 32 (over y, x, core), head: 8 (over z).
Axes of the slice: x: 4, y: 4, z: 8, core: 2. Of those that a mesh axis runs over, the one named last changes fastest.
Arguments:
- query_rows: bfloat16 [16384, 4096], P('seq', 'head'), may hold values from -6 to 6
- key_rows: bfloat16 [16384, 4096], P('seq', 'head'), may hold values from -6 to 6
- value_rows: bfloat16 [16384, 4096], P('seq', 'head'), may hold values from -6 to 6
- out_weight: bfloat16 [4096, 4096], P('seq', 'head'), may hold values from -0.09375 to 0.09375
- target_rows: bfloat16 [16384, 4096], P('seq', 'head'), may hold values from -6 to 6
Outputs:
- output: bfloat16 [16384, 4096], P('seq', 'head')
- grad_query: bfloat16 [16384, 4096], P('seq', 'head')
- grad_key: bfloat16 [16384, 4096], P('seq', 'head')
- grad_value: bfloat16 [16384, 4096], P('seq', 'head')
- grad_weight: float32 [4096, 4096], P('seq', 'head')
All inputs are finite; a program needn't handle non-finite values.
Results may differ from a plain program's by a relative error of at most 0.019.
Values may be sent and summed in bfloat16 or wider, within the bound.
A program may use at most 64 MiB of HBM per device.

v0:
```python
import math
import jax
import jax.numpy as jnp
from jax import lax
from jax.sharding import Mesh
from jax.sharding import PartitionSpec as P

DH = 128
BLK = 512
SEQ = ("seq_0", "seq_1", "seq_2")
EXACT = lax.Precision.HIGHEST


def filled_with(x, identity):
    return jnp.broadcast_to(jnp.asarray(identity, x.dtype), x.shape)


def entering(x, axes, combine, identity, reverse):
    before = start = filled_with(x, identity)
    so_far = x
    for axis in reversed(axes):
        devices, place = (lax.axis_size(axis), lax.axis_index(axis))
        pieces = lax.all_gather(so_far.astype(jnp.bfloat16), axis)
        inside, so_far = (start, start)
        for k in reversed(range(devices)) if reverse else range(devices):
            passed = k > place if reverse else k < place
            so_far = combine(so_far, pieces[k].astype(x.dtype))
            inside = jnp.where(passed, so_far, inside)
        before = combine(inside, before)
    return before


def add_states(earlier, later_one):
    return earlier + later_one


def on_device(query_rows, key_rows, value_rows, out_weight, target_rows):
    rows_dev = query_rows.shape[0]
    feature_width = query_rows.shape[1]
    local_heads = feature_width // DH
    block_count = rows_dev // BLK
    seq_count = lax.axis_size(SEQ)
    total_rows = rows_dev * seq_count
    seq_index = lax.axis_index(SEQ)
    positions = (seq_index * rows_dev + jnp.arange(rows_dev, dtype=jnp.int32) + 1).astype(
        jnp.float32
    )
    query_scale = lax.rsqrt(jnp.float32(DH) * positions)
    scaled = (query_rows.astype(jnp.float32) * query_scale[:, None]).astype(jnp.bfloat16)
    shaped = (block_count, BLK, local_heads, DH)
    query_blocks = scaled.reshape(shaped)
    key_blocks = key_rows.reshape(shaped)
    value_blocks = value_rows.reshape(shaped)
    causal = jnp.tril(jnp.ones((BLK, BLK), dtype=bool))
    empty_state = jnp.zeros((local_heads, DH, DH), jnp.float32)
    block_kv = jnp.einsum(
        "bshd,bshe->bhde", key_blocks, value_blocks, preferred_element_type=jnp.float32
    )
    local_total = jnp.sum(block_kv, axis=0)
    earlier = entering(local_total, SEQ, add_states, empty_state, False)
    running_kv = jnp.cumsum(block_kv, axis=0)
    before = earlier[None] + jnp.concatenate([jnp.zeros_like(block_kv), running_kv[:-1]], axis=0)
    inter = jnp.einsum("bthd,bhde->bthe", query_blocks.astype(jnp.float32), before, precision=EXACT)
    scores = jnp.einsum(
        "bthd,bshd->bhts", query_blocks, key_blocks, preferred_element_type=jnp.float32
    )
    scores = jnp.where(causal, scores, 0.0).astype(jnp.bfloat16)
    intra = jnp.einsum("bhts,bshe->bthe", scores, value_blocks, preferred_element_type=jnp.float32)
    attended = (inter + intra).astype(jnp.bfloat16).reshape(rows_dev, feature_width)
    whole_weight = lax.all_gather(out_weight, SEQ, axis=0, tiled=True)
    partial_out = lax.dot_general(
        attended, whole_weight, (((1,), (1,)), ((), ())), preferred_element_type=jnp.float32
    )
    summed = lax.psum_scatter(
        partial_out.astype(jnp.bfloat16), "head", scatter_dimension=1, tiled=True
    )
    residual = (summed.astype(jnp.float32) - target_rows.astype(jnp.float32)).astype(jnp.bfloat16)
    residual_full = lax.all_gather(residual, "head", axis=1, tiled=True)
    grad_attended = jnp.dot(residual_full, whole_weight, preferred_element_type=jnp.float32).astype(
        jnp.bfloat16
    )
    weight_factor = 1.0 / math.sqrt(total_rows)
    product = lax.dot_general(
        residual_full, attended, (((0,), (0,)), ((), ())), preferred_element_type=jnp.float32
    )
    grad_weight = lax.psum_scatter(
        (product * weight_factor).astype(jnp.bfloat16), SEQ, scatter_dimension=0, tiled=True
    ).astype(jnp.float32)
    grad_blocks = grad_attended.reshape(shaped)
    block_qg = jnp.einsum(
        "bthd,bthe->bhde", query_blocks, grad_blocks, preferred_element_type=jnp.float32
    )
    local_grad = jnp.sum(block_qg, axis=0)
    later = entering(local_grad, SEQ, add_states, empty_state, True)
    running_qg = jnp.cumsum(block_qg[::-1], axis=0)[::-1]
    after = later[None] + jnp.concatenate([running_qg[1:], jnp.zeros_like(block_qg)], axis=0)
    mixed = jnp.einsum(
        "bthe,bshe->bhts", grad_blocks, value_blocks, preferred_element_type=jnp.float32
    )
    mixed = jnp.where(causal, mixed, 0.0).astype(jnp.bfloat16)
    grad_scaled = jnp.einsum(
        "bthe,bhde->bthd", grad_blocks.astype(jnp.float32), before, precision=EXACT
    )
    grad_scaled = grad_scaled + jnp.einsum(
        "bhts,bshd->bthd", mixed, key_blocks, preferred_element_type=jnp.float32
    )
    grad_key = jnp.einsum(
        "bshe,bhde->bshd", value_blocks.astype(jnp.float32), after, precision=EXACT
    )
    grad_key = grad_key + jnp.einsum(
        "bhts,bthd->bshd", mixed, query_blocks, preferred_element_type=jnp.float32
    )
    grad_value = jnp.einsum(
        "bshd,bhde->bshe", key_blocks.astype(jnp.float32), after, precision=EXACT
    )
    grad_value = grad_value + jnp.einsum(
        "bhts,bthe->bshe", scores, grad_blocks, preferred_element_type=jnp.float32
    )
    grad_query = (grad_scaled.reshape(rows_dev, feature_width) * query_scale[:, None]).astype(
        jnp.bfloat16
    )
    return (
        summed,
        grad_query,
        grad_key.astype(jnp.bfloat16).reshape(rows_dev, feature_width),
        grad_value.astype(jnp.bfloat16).reshape(rows_dev, feature_width),
        grad_weight,
    )


def solution(mesh):
    torus = Mesh(
        mesh.devices.reshape(4, 4, 2, mesh.shape["head"]), ("seq_0", "seq_1", "seq_2", "head")
    )
    return jax.shard_map(
        on_device,
        mesh=torus,
        in_specs=(P(SEQ, "head"), P(SEQ, "head"), P(SEQ, "head"), P(SEQ, "head"), P(SEQ, "head")),
        out_specs=(P(SEQ, "head"), P(SEQ, "head"), P(SEQ, "head"), P(SEQ, "head"), P(SEQ, "head")),
        check_vma=False,
    )
```

profile of v0, /device:TPU:2, one launch (start us, length us, event | category | flops | bytes accessed | tf_op | source)
XLA Modules:
  0.0 285.8 jit_solution(8579663501388462409)
XLA Ops:
  7.2 0.0 copy-start
  7.2 0.0 all-gather.5.cloned.1.call-start
  7.2 0.7 all-gather.5.cloned.1.call-update
  7.9 0.0 reduce-scatter.3.cloned.1.call-start
  8.0 1.3 copy.82
  9.3 1.4 multiply_convert_fusion.2
  10.7 0.2 copy.55
  10.9 0.3 convolution_convert_fusion.3
  11.2 2.0 all-gather
  13.2 0.1 iota_compare_fusion
  13.3 12.8 %all_gather.31 = bf16[4,4,128,128]{3,2,1,0:T(8,128)(2,1)S(1)} all-gather(bf16[1,4,128,128]{3,2,1,0:T(8,128)(2,1)S(1)} %fusion.41), channel_id=1, replica_groups=mesh['seq_0'=4,'seq_1'=4,'seq_2'=2,'head'=8] {'seq_1'}, dimensions={0}, use_global_device_ids=true | all-gather | bytes 655360 | tf_op jit(solution)/shard_map/all_gather | solution.py:23
  26.2 0.1 fusion.40
  26.2 15.3 %all_gather.32 = bf16[4,4,128,128]{3,2,1,0:T(8,128)(2,1)S(1)} all-gather(bf16[1,4,128,128]{3,2,1,0:T(8,128)(2,1)S(1)} %fusion.40), channel_id=1, replica_groups=mesh['seq_0'=4,'seq_1'=4,'seq_2'=2,'head'=8] {'seq_0'}, dimensions={0}, use_global_device_ids=true | all-gather | bytes 655360 | tf_op jit(solution)/shard_map/all_gather | solution.py:23
  41.6 0.3 fusion.20
  41.8 2.0 select_convert_fusion.1
  43.8 0.8 convolution_bitcast_fusion.1
  44.7 1.4 fusion
  46.1 18.6 %all-gather.5.cloned.1.call-done = bf16[4096,512]{1,0:T(8,128)(2,1)} async-done(((bf16[128,512]{1,0:T(8,128)(2,1)}), bf16[4096,512]{1,0:T(8,128)(2,1)}) %all-gather.5.cloned.1.call-update) | async-done | bytes 4194320 | tf_op jit(solution)/shard_map/all_gather | solution.py:70
  64.7 6.7 %convolution_convert_fusion = bf16[512,4096]{1,0:T(8,128)(2,1)} fusion(bf16[512,512]{0,1:T(8,128)(2,1)} %bitcast.114, bf16[4096,512]{1,0:T(8,128)(2,1)} %all-gather.5.cloned.1.call-done), kind=kOutput, calls=%fused_computation.1 | convolution fusion | flops 2149580800 | bytes 8912896 | tf_op jit(solution)/shard_map/dot_general | solution.py:71
  71.5 0.0 reduce-scatter.3.cloned.1.call-update
  71.5 0.0 all-gather.7.cloned.1.call-start
  71.5 55.2 %reduce-scatter.3.cloned.1.call-done = bf16[512,512]{1,0:T(8,128)(2,1)} async-done(((bf16[512,4096]{1,0:T(8,128)(2,1)}), bf16[512,512]{1,0:T(8,128)(2,1)}) %reduce-scatter.3.cloned.1.call-update) | async-done | bytes 524304 | tf_op jit(solution)/shard_map/reduce_scatter | solution.py:74
  126.7 2.1 subtract_convert_fusion
  128.9 0.0 all-gather.7.cloned.1.call-update
  128.9 0.0 reduce-scatter.5.cloned.1.call-start
  128.9 53.6 %all-gather.7.cloned.1.call-done = bf16[512,4096]{1,0:T(8,128)(2,1)} async-done(((bf16[512,512]{1,0:T(8,128)(2,1)}), bf16[512,4096]{1,0:T(8,128)(2,1)}) %all-gather.7.cloned.1.call-update) | async-done | bytes 4194320 | tf_op jit(solution)/shard_map/all_gather | solution.py:78
  182.5 6.7 %multiply_convert_fusion = bf16[4096,512]{1,0:T(8,128)(2,1)} fusion(bf16[512,4096]{1,0:T(8,128)(2,1)} %all-gather.7.cloned.1.call-done, bf16[512,512]{0,1:T(8,128)(2,1)} %bitcast.115), kind=kOutput, calls=%fused_computation | convolution fusion | flops 2151677952 | bytes 8912896 | tf_op jit(solution)/shard_map/dot_general | solution.py:83
  189.2 0.0 reduce-scatter.5.cloned.1.call-update
  189.3 5.8 %convolution_convert_fusion.1 = bf16[512,512]{0,1:T(8,128)(2,1)S(1)} fusion(bf16[512,4096]{1,0:T(8,128)(2,1)} %all-gather.7.cloned.1.call-done, bf16[4096,512]{1,0:T(8,128)(2,1)} %all-gather.5.cloned.1.call-done), kind=kOutput, calls=%fused_computation.10 | convolution fusion | flops 2147745792 | bytes 8912896 | tf_op jit(solution)/shard_map/dot_general | solution.py:79
  195.1 0.3 convolution_convert_fusion.2
  195.4 2.1 all-gather.1
  197.6 13.5 %all_gather.36 = bf16[4,4,128,128]{3,2,1,0:T(8,128)(2,1)S(1)} all-gather(bf16[1,4,128,128]{3,2,1,0:T(8,128)(2,1)S(1)} %fusion.42), channel_id=1, replica_groups=mesh['seq_0'=4,'seq_1'=4,'seq_2'=2,'head'=8] {'seq_1'}, dimensions={0}, use_global_device_ids=true | all-gather | bytes 655360 | tf_op jit(solution)/shard_map/all_gather | solution.py:23
  211.1 0.1 fusion.39
  211.2 13.5 %all_gather.37 = bf16[4,4,128,128]{3,2,1,0:T(8,128)(2,1)S(1)} all-gather(bf16[1,4,128,128]{3,2,1,0:T(8,128)(2,1)S(1)} %fusion.39), channel_id=1, replica_groups=mesh['seq_0'=4,'seq_1'=4,'seq_2'=2,'head'=8] {'seq_0'}, dimensions={0}, use_global_device_ids=true | all-gather | bytes 655360 | tf_op jit(solution)/shard_map/all_gather | solution.py:23
  224.7 0.3 fusion.29
  224.9 0.4 fusion.44
  225.4 0.6 fusion.2
  226.0 1.0 copy.49
  227.0 1.9 select_convert_fusion
  229.0 0.4 fusion.43
  229.4 1.4 fusion.1
  230.8 2.1 copy.48
  232.9 1.8 convolution_bitcast_fusion
  234.8 0.6 convolution_add_fusion.2
  235.4 0.3 copy.41
  235.7 0.9 multiply_convert_fusion.1
  236.7 41.0 %reduce-scatter.5.cloned.1.call-done = bf16[128,512]{1,0:T(8,128)(2,1)} async-done(((bf16[4096,512]{1,0:T(8,128)(2,1)}), bf16[128,512]{1,0:T(8,128)(2,1)}) %reduce-scatter.5.cloned.1.call-update) | async-done | bytes 131088 | tf_op jit(solution)/shard_map/reduce_scatter | solution.py:86
  277.6 1.6 convert_element_type.247
  (18 shorter events, 0.1 us)
Async XLA Ops:
  7.2 3.7 %copy-start = (bf16[512,512]{1,0:T(8,128)(2,1)S(1)}, bf16[512,512]{1,0:T(8,128)(2,1)}, u32[]{:S(2)}) copy-start(bf16[512,512]{1,0:T(8,128)(2,1)} %param.7) | copy-start | bytes 1572868
  7.2 57.6 %all-gather.5.cloned.1.call-start = ((), (), s32[]{:S(2)}) async-start(), calls=%async_computation.2 | async-start | bytes 4325376 | tf_op jit(solution)/shard_map/all_gather | solution.py:70
  7.9 118.8 %reduce-scatter.3.cloned.1.call-start = ((), (), s32[]{:S(2)}) async-start(), calls=%async_computation.3 | async-start | bytes 4718592 | tf_op jit(solution)/shard_map/reduce_scatter | solution.py:74
  9.2 32.6 %copy-start.5 = (bf16[512,512]{0,1:T(8,128)(2,1)}, bf16[512,512]{0,1:T(8,128)(2,1)S(1)}, u32[]{:S(2)}) copy-start(bf16[512,512]{0,1:T(8,128)(2,1)S(1)} %copy.82) | copy-start | bytes 1572868
  13.3 31.4 %copy-start.7 = (pred[512,512]{1,0:T(8,128)(4,1)}, pred[512,512]{1,0:T(8,128)(4,1)S(1)}, u32[]{:S(2)}) copy-start(pred[512,512]{1,0:T(8,128)(4,1)S(1)} %iota_compare_fusion) | copy-start | bytes 786436
  41.8 2.8 copy-start.3
  71.5 111.0 %all-gather.7.cloned.1.call-start = ((), (), s32[]{:S(2)}) async-start(), calls=%async_computation.4 | async-start | bytes 4718592 | tf_op jit(solution)/shard_map/all_gather | solution.py:78
  128.9 148.8 %reduce-scatter.5.cloned.1.call-start = ((), (), s32[]{:S(2)}) async-start(), calls=%async_computation.5 | async-start | bytes 4325376 | tf_op jit(solution)/shard_map/reduce_scatter | solution.py:86
  195.1 30.3 %copy-start.1 = (bf16[512,512]{0,1:T(8,128)(2,1)}, bf16[512,512]{0,1:T(8,128)(2,1)S(1)}, u32[]{:S(2)}) copy-start(bf16[512,512]{0,1:T(8,128)(2,1)S(1)} %convolution_convert_fusion.1) | copy-start | bytes 1572868
  195.4 30.0 %copy-start.6 = (bf16[512,512]{1,0:T(8,128)(2,1)S(1)}, bf16[512,512]{1,0:T(8,128)(2,1)}, u32[]{:S(2)}) copy-start(bf16[512,512]{1,0:T(8,128)(2,1)} %param.6) | copy-start | bytes 1572868
  229.4 5.3 %copy-start.2 = (bf16[512,512]{0,1:T(8,128)(2,1)S(1)}, bf16[512,512]{0,1:T(8,128)(2,1)}, u32[]{:S(2)}) copy-start(bf16[512,512]{0,1:T(8,128)(2,1)} %copy-done.1) | copy-start | bytes 1572868
  230.8 4.0 %copy-start.4 = (f32[4,128,128]{2,1,0:T(8,128)S(1)}, f32[4,128,128]{2,1,0:T(8,128)}, u32[]{:S(2)}) copy-start(f32[4,128,128]{2,1,0:T(8,128)} %copy-done.3) | copy-start | bytes 786436
Sparse Core Ops, SparseCore 0:
  10.5 54.1 all-gather.4
  71.6 55.0 reduce-scatter.2
  129.1 53.3 all-gather.6
  189.3 88.2 reduce-scatter.4
where the time goes:
time: 286 us
  waiting for transfers between devices  169 us (59%)
  blocking collectives  59.3 us (21%)
  matrix products  31.3 us (11%)
  between operations  14.1 us (5%)
  other arithmetic  6.88 us (2%)
  local copies, waits for them, and re-layouts  4.94 us (2%)
    all_gather x6, blocking collectives, entering(): pieces = lax.all_gather(so_far.astype(jnp.bfloat16), axis)  59.3 us
    reduce_scatter x1, waiting for transfers between devices, on_device(): lax.psum_scatter(partial_out.astype(jnp.bfloat16), 'head', scatter_dimens...  55.2 us
    all_gather x1, waiting for transfers between devices, on_device(): residual_full = lax.all_gather(residual, 'head', axis=1, tiled=True)  53.6 us
    reduce_scatter x1, waiting for transfers between devices, on_device(): lax.psum_scatter((product * weight_factor).astype(jnp.bfloat16), SEQ, sca...  41 us
    all_gather x1, waiting for transfers between devices, on_device(): whole_weight = lax.all_gather(out_weight, SEQ, axis=0, tiled=True)  18.6 us
    dot_general x1, matrix products, on_device(): lax.dot_general(attended, whole_weight, (((1,), (1,)), ((), ())), preferr...  6.73 us
    dot_general x1, matrix products, on_device(): lax.dot_general(residual_full, attended, (((0,), (0,)), ((), ())), prefer...  6.68 us
    dot_general x1, matrix products, on_device(): jnp.dot(residual_full, whole_weight, preferred_element_type=jnp.float32)  5.84 us
  transfers between devices with their start and end apart: 4, of which 4 were waited for; matrix products, arithmetic and copies ran while one was open for 9% of the time, Pallas kernels for 0%

commit v1 on v0

--- a/solution.py
+++ b/solution.py
@@ -75,7 +75,12 @@
         partial_out.astype(jnp.bfloat16), "head", scatter_dimension=1, tiled=True
     )
     residual = (summed.astype(jnp.float32) - target_rows.astype(jnp.float32)).astype(jnp.bfloat16)
-    residual_full = lax.all_gather(residual, "head", axis=1, tiled=True)
+    ring = [residual]
+    for hop in range(7):
+        ring.append(lax.ppermute(ring[-1], "head", [(dev, (dev + 1) % 8) for dev in range(8)]))
+    residual_full = jnp.roll(
+        jnp.concatenate(ring[::-1], axis=1), (lax.axis_index("head") + 1) * ring[0].shape[1], axis=1
+    )
     grad_attended = jnp.dot(residual_full, whole_weight, preferred_element_type=jnp.float32).astype(
         jnp.bfloat16
     )

time: 286 us -> 338 us (1.18)
  waiting for transfers between devices: 169 us -> 204 us
  local copies, waits for them, and re-layouts: 4.94 us -> 23.4 us
    ppermute x0 -> x7, waiting for transfers between devices: none -> 87.9 us  [on_device(): lax.ppermute(ring[-1], 'head', [(dev, (dev + 1) % 8) for dev in range(8)])]
    all_gather x1 -> x0, waiting for transfers between devices: 53.6 us -> none  [on_device(): residual_full = lax.all_gather(residual, 'head', axis=1, tiled=True)]
    unnamed x18 -> x57, local copies, waits for them, and re-layouts: 3.14 us -> 21.6 us
  transfers between devices with their start and end apart: 4 -> 10, of which waited for: 4 -> 10; matrix products, arithmetic and copies ran while one was open for 9% -> 7% of each run, Pallas kernels for 0% -> 0%
where the time goes in v1:
time: 338 us; the launch traced here: 337 us
  waiting for transfers between devices  204 us (60%)
  blocking collectives  59.1 us (17%)
  matrix products  29.3 us (9%)
  local copies, waits for them, and re-layouts  23.4 us (7%)
  between operations  14.3 us (4%)
  other arithmetic  6.09 us (2%)
    ppermute x7, waiting for transfers between devices, on_device(): lax.ppermute(ring[-1], 'head', [(dev, (dev + 1) % 8) for dev in range(8)])  87.9 us
    all_gather x6, blocking collectives, entering(): pieces = lax.all_gather(so_far.astype(jnp.bfloat16), axis)  59.1 us
    reduce_scatter x1, waiting for transfers between devices, on_device(): lax.psum_scatter(partial_out.astype(jnp.bfloat16), 'head', scatter_dimens...  55.2 us
    reduce_scatter x1, waiting for transfers between devices, on_device(): lax.psum_scatter((product * weight_factor).astype(jnp.bfloat16), SEQ, sca...  42 us
    unnamed x57, local copies, waits for them, and re-layouts  21.6 us
    all_gather x1, waiting for transfers between devices, on_device(): whole_weight = lax.all_gather(out_weight, SEQ, axis=0, tiled=True)  18.7 us
  transfers between devices with their start and end apart: 10, of which 10 were waited for; matrix products, arithmetic and copies ran while one was open for 7% of the time, Pallas kernels for 0%

profile of v1, /device:TPU:2, one launch (start us, length us, event | category | flops | bytes accessed | tf_op | source)
XLA Modules:
  0.0 336.8 jit_solution(2920218646783849766)
XLA Ops:
  8.0 1.3 copy.82
  9.3 1.4 multiply_convert_fusion.2
  11.2 2.0 all-gather
  13.3 12.8 %all_gather.28 = bf16[4,4,128,128]{3,2,1,0:T(8,128)(2,1)S(1)} all-gather(bf16[1,4,128,128]{3,2,1,0:T(8,128)(2,1)S(1)} %fusion.47), channel_id=1, replica_groups=mesh['seq_0'=4,'seq_1'=4,'seq_2'=2,'head'=8] {'seq_1'}, dimensions={0}, use_global_device_ids=true | all-gather | bytes 655360 | tf_op jit(solution)/shard_map/all_gather | solution.py:23
  26.3 15.3 %all_gather.29 = bf16[4,4,128,128]{3,2,1,0:T(8,128)(2,1)S(1)} all-gather(bf16[1,4,128,128]{3,2,1,0:T(8,128)(2,1)S(1)} %fusion.46), channel_id=1, replica_groups=mesh['seq_0'=4,'seq_1'=4,'seq_2'=2,'head'=8] {'seq_0'}, dimensions={0}, use_global_device_ids=true | all-gather | bytes 655360 | tf_op jit(solution)/shard_map/all_gather | solution.py:23
  41.8 2.0 select_convert_fusion.1
  43.8 0.8 convolution_bitcast_fusion.1
  44.6 1.4 fusion.6
  46.1 18.7 %all-gather.4.cloned.1.call-done = bf16[4096,512]{1,0:T(8,128)(2,1)} async-done(((bf16[128,512]{1,0:T(8,128)(2,1)}), bf16[4096,512]{1,0:T(8,128)(2,1)}) %all-gather.4.cloned.1.call-update) | async-done | bytes 4194320 | tf_op jit(solution)/shard_map/all_gather | solution.py:70
  64.8 6.7 %convolution_convert_fusion = bf16[512,4096]{1,0:T(8,128)(2,1)} fusion(bf16[512,512]{0,1:T(8,128)(2,1)} %bitcast.112, bf16[4096,512]{1,0:T(8,128)(2,1)} %all-gather.4.cloned.1.call-done), kind=kOutput, calls=%fused_computation.1 | convolution fusion | flops 2149580800 | bytes 8912896 | tf_op jit(solution)/shard_map/dot_general | solution.py:71
  71.6 55.2 %reduce-scatter.3.cloned.1.call-done = bf16[512,512]{1,0:T(8,128)(2,1)} async-done(((bf16[512,4096]{1,0:T(8,128)(2,1)}), bf16[512,512]{1,0:T(8,128)(2,1)}) %reduce-scatter.3.cloned.1.call-update) | async-done | bytes 524304 | tf_op jit(solution)/shard_map/reduce_scatter | solution.py:74
  126.7 1.3 subtract_convert_fusion
  128.1 0.9 copy-done.1
  129.0 14.8 %collective-permute-done = bf16[512,512]{1,0:T(8,128)(2,1)S(1)} collective-permute-done((bf16[512,512]{1,0:T(8,128)(2,1)S(1)}, bf16[512,512]{1,0:T(8,128)(2,1)S(1)}, u32[]{:S(2)}, u32[]{:S(2)}) %collective-permute-start) | collective-permute-done | bytes 524320 | tf_op jit(solution)/shard_map/ppermute | solution.py:80
  144.5 13.9 %collective-permute-done.1 = bf16[512,512]{1,0:T(8,128)(2,1)S(1)} collective-permute-done((bf16[512,512]{1,0:T(8,128)(2,1)S(1)}, bf16[512,512]{1,0:T(8,128)(2,1)S(1)}, u32[]{:S(2)}, u32[]{:S(2)}) %collective-permute-start.1) | collective-permute-done | bytes 524320 | tf_op jit(solution)/shard_map/ppermute | solution.py:80
  158.5 0.8 copy-done.8
  159.3 13.1 %collective-permute-done.2 = bf16[512,512]{1,0:T(8,128)(2,1)S(1)} collective-permute-done((bf16[512,512]{1,0:T(8,128)(2,1)S(1)}, bf16[512,512]{1,0:T(8,128)(2,1)S(1)}, u32[]{:S(2)}, u32[]{:S(2)}) %collective-permute-start.2) | collective-permute-done | bytes 524320 | tf_op jit(solution)/shard_map/ppermute | solution.py:80
  172.3 0.8 copy-done.10
  173.2 12.2 %collective-permute-done.3 = bf16[512,512]{1,0:T(8,128)(2,1)S(1)} collective-permute-done((bf16[512,512]{1,0:T(8,128)(2,1)S(1)}, bf16[512,512]{1,0:T(8,128)(2,1)S(1)}, u32[]{:S(2)}, u32[]{:S(2)}) %collective-permute-start.3) | collective-permute-done | bytes 524320 | tf_op jit(solution)/shard_map/ppermute | solution.py:80
  185.4 0.8 copy-done.12
  186.2 11.4 %collective-permute-done.4 = bf16[512,512]{1,0:T(8,128)(2,1)S(1)} collective-permute-done((bf16[512,512]{1,0:T(8,128)(2,1)S(1)}, bf16[512,512]{1,0:T(8,128)(2,1)S(1)}, u32[]{:S(2)}, u32[]{:S(2)}) %collective-permute-start.4) | collective-permute-done | bytes 524320 | tf_op jit(solution)/shard_map/ppermute | solution.py:80
  197.5 0.8 copy-done.14
  198.3 11.9 %collective-permute-done.5 = bf16[512,512]{1,0:T(8,128)(2,1)} collective-permute-done((bf16[512,512]{1,0:T(8,128)(2,1)S(1)}, bf16[512,512]{1,0:T(8,128)(2,1)}, u32[]{:S(2)}, u32[]{:S(2)}) %collective-permute-start.5) | collective-permute-done | bytes 524320 | tf_op jit(solution)/shard_map/ppermute | solution.py:80
  210.3 10.6 %collective-permute-done.6 = bf16[512,512]{1,0:T(8,128)(2,1)} collective-permute-done((bf16[512,512]{1,0:T(8,128)(2,1)}, bf16[512,512]{1,0:T(8,128)(2,1)}, u32[]{:S(2)}, u32[]{:S(2)}) %collective-permute-start.6) | collective-permute-done | bytes 524320 | tf_op jit(solution)/shard_map/ppermute | solution.py:80
  220.9 1.1 constant_dynamic-update-slice_fusion.15
  222.0 1.1 constant_dynamic-update-slice_fusion.14
  223.1 1.1 constant_dynamic-update-slice_fusion.13
  224.3 1.1 constant_dynamic-update-slice_fusion.12
  225.4 1.1 constant_dynamic-update-slice_fusion.11
  226.5 1.1 constant_dynamic-update-slice_fusion.10
  227.6 1.1 constant_dynamic-update-slice_fusion.9
  228.7 1.1 constant_dynamic-update-slice_fusion.8
  229.8 1.1 constant_dynamic-update-slice_fusion.7
  231.0 1.1 constant_dynamic-update-slice_fusion.6
  232.5 3.3 copy-done.19
  235.8 4.4 %multiply_convert_fusion = bf16[4096,512]{1,0:T(8,128)(2,1)} fusion(bf16[512,512]{0,1:T(8,128)(2,1)S(1)} %bitcast.113, bf16[512,8192]{1,0:T(8,128)(2,1)S(1)} %constant_dynamic-update-slice_fusion, s32[]{:T(128)S(6)} %select_n.188), kind=kOutput, calls=%fused_computation | convolution fusion | flops 2151677952 | bytes 8912900 | tf_op jit(solution)/shard_map/dot_general | solution.py:88
  240.2 5.8 %fusion.3 = bf16[512,512]{0,1:T(8,128)(2,1)S(1)} fusion(bf16[4096,512]{1,0:T(8,128)(2,1)} %all-gather.4.cloned.1.call-done, bf16[512,8192]{1,0:T(8,128)(2,1)} %copy-done.19, s32[]{:T(128)S(6)} %select_n.188), kind=kOutput, calls=%fused_computation.13 | convolution fusion | flops 2147745792 | bytes 8912900 | tf_op jit(solution)/shard_map/dot_general | solution.py:84
  246.4 2.1 all-gather.1
  248.6 13.6 %all_gather.32 = bf16[4,4,128,128]{3,2,1,0:T(8,128)(2,1)S(1)} all-gather(bf16[1,4,128,128]{3,2,1,0:T(8,128)(2,1)S(1)} %fusion.48), channel_id=1, replica_groups=mesh['seq_0'=4,'seq_1'=4,'seq_2'=2,'head'=8] {'seq_1'}, dimensions={0}, use_global_device_ids=true | all-gather | bytes 655360 | tf_op jit(solution)/shard_map/all_gather | solution.py:23
  262.2 13.2 %all_gather.33 = bf16[4,4,128,128]{3,2,1,0:T(8,128)(2,1)S(1)} all-gather(bf16[1,4,128,128]{3,2,1,0:T(8,128)(2,1)S(1)} %fusion.45), channel_id=1, replica_groups=mesh['seq_0'=4,'seq_1'=4,'seq_2'=2,'head'=8] {'seq_0'}, dimensions={0}, use_global_device_ids=true | all-gather | bytes 655360 | tf_op jit(solution)/shard_map/all_gather | solution.py:23
  276.8 1.0 copy.49
  277.8 1.9 select_convert_fusion
  280.8 1.0 copy.48
  281.8 1.8 convolution_bitcast_fusion
  283.7 1.7 convolution_add_fusion.2
  285.7 0.9 multiply_convert_fusion.1
  286.7 42.0 %reduce-scatter.5.cloned.1.call-done = bf16[128,512]{1,0:T(8,128)(2,1)} async-done(((bf16[4096,512]{1,0:T(8,128)(2,1)}), bf16[128,512]{1,0:T(8,128)(2,1)}) %reduce-scatter.5.cloned.1.call-update) | async-done | bytes 131088 | tf_op jit(solution)/shard_map/reduce_scatter | solution.py:91
  328.7 1.6 convert_element_type.247
  (69 shorter events, 6.1 us)
Async XLA Ops:
  7.2 3.7 %copy-start = (bf16[512,512]{1,0:T(8,128)(2,1)S(1)}, bf16[512,512]{1,0:T(8,128)(2,1)}, u32[]{:S(2)}) copy-start(bf16[512,512]{1,0:T(8,128)(2,1)} %param.7) | copy-start | bytes 1572868
  7.2 57.6 %all-gather.4.cloned.1.call-start = ((), (), s32[]{:S(2)}) async-start(), calls=%async_computation.2 | async-start | bytes 4325376 | tf_op jit(solution)/shard_map/all_gather | solution.py:70
  7.9 118.8 %reduce-scatter.3.cloned.1.call-start = ((), (), s32[]{:S(2)}) async-start(), calls=%async_computation.3 | async-start | bytes 4718592 | tf_op jit(solution)/shard_map/reduce_scatter | solution.py:74
  9.2 1.6 copy-start.5
  13.3 28.6 %copy-start.18 = (pred[512,512]{1,0:T(8,128)(4,1)}, pred[512,512]{1,0:T(8,128)(4,1)S(1)}, u32[]{:S(2)}) copy-start(pred[512,512]{1,0:T(8,128)(4,1)S(1)} %iota_compare_fusion) | copy-start | bytes 786436
  41.8 2.8 copy-start.4
  71.5 257.2 %reduce-scatter.5.cloned.1.call-start = ((), (), s32[]{:S(2)}) async-start(), calls=%async_computation.4 | async-start | bytes 4325376 | tf_op jit(solution)/shard_map/reduce_scatter | solution.py:91
  128.1 0.9 copy-start.1
  129.0 14.8 %collective-permute-start = (bf16[512,512]{1,0:T(8,128)(2,1)S(1)}, bf16[512,512]{1,0:T(8,128)(2,1)S(1)}, u32[]{:S(2)}, u32[]{:S(2)}) collective-permute-start(bf16[512,512]{1,0:T(8,128)(2,1)S(1)} %subtract_convert_fusion), channel_id=1, source_target_pairs={{0,1},{1,2},{2,3},{3,4},{4,5},{5,6},{6,7},{7,0},{8,9},{9,10},{10,1... | collective-permute-start | bytes 1572872 | tf_op jit(solution)/shard_map/ppermute | solution.py:80
  143.7 0.8 copy-start.6
  144.5 13.9 %collective-permute-start.1 = (bf16[512,512]{1,0:T(8,128)(2,1)S(1)}, bf16[512,512]{1,0:T(8,128)(2,1)S(1)}, u32[]{:S(2)}, u32[]{:S(2)}) collective-permute-start(bf16[512,512]{1,0:T(8,128)(2,1)S(1)} %collective-permute-done), channel_id=1, source_target_pairs={{0,1},{1,2},{2,3},{3,4},{4,5},{5,6},{6,7},{7,0},{8,9},{9,10},{10,1... | collective-permute-start | bytes 1572872 | tf_op jit(solution)/shard_map/ppermute | solution.py:80
  158.5 0.8 copy-start.8
  159.3 13.1 %collective-permute-start.2 = (bf16[512,512]{1,0:T(8,128)(2,1)S(1)}, bf16[512,512]{1,0:T(8,128)(2,1)S(1)}, u32[]{:S(2)}, u32[]{:S(2)}) collective-permute-start(bf16[512,512]{1,0:T(8,128)(2,1)S(1)} %collective-permute-done.1), channel_id=1, source_target_pairs={{0,1},{1,2},{2,3},{3,4},{4,5},{5,6},{6,7},{7,0},{8,9},{9,10},{10,1... | collective-permute-start | bytes 1572872 | tf_op jit(solution)/shard_map/ppermute | solution.py:80
  172.3 0.8 copy-start.10
  173.2 12.2 %collective-permute-start.3 = (bf16[512,512]{1,0:T(8,128)(2,1)S(1)}, bf16[512,512]{1,0:T(8,128)(2,1)S(1)}, u32[]{:S(2)}, u32[]{:S(2)}) collective-permute-start(bf16[512,512]{1,0:T(8,128)(2,1)S(1)} %collective-permute-done.2), channel_id=1, source_target_pairs={{0,1},{1,2},{2,3},{3,4},{4,5},{5,6},{6,7},{7,0},{8,9},{9,10},{10,1... | collective-permute-start | bytes 1572872 | tf_op jit(solution)/shard_map/ppermute | solution.py:80
  185.4 0.8 copy-start.12
  186.2 11.4 %collective-permute-start.4 = (bf16[512,512]{1,0:T(8,128)(2,1)S(1)}, bf16[512,512]{1,0:T(8,128)(2,1)S(1)}, u32[]{:S(2)}, u32[]{:S(2)}) collective-permute-start(bf16[512,512]{1,0:T(8,128)(2,1)S(1)} %collective-permute-done.3), channel_id=1, source_target_pairs={{0,1},{1,2},{2,3},{3,4},{4,5},{5,6},{6,7},{7,0},{8,9},{9,10},{10,1... | collective-permute-start | bytes 1572872 | tf_op jit(solution)/shard_map/ppermute | solution.py:80
  197.5 0.8 copy-start.14
  198.3 11.9 %collective-permute-start.5 = (bf16[512,512]{1,0:T(8,128)(2,1)S(1)}, bf16[512,512]{1,0:T(8,128)(2,1)}, u32[]{:S(2)}, u32[]{:S(2)}) collective-permute-start(bf16[512,512]{1,0:T(8,128)(2,1)S(1)} %collective-permute-done.4), channel_id=1, source_target_pairs={{0,1},{1,2},{2,3},{3,4},{4,5},{5,6},{6,7},{7,0},{8,9},{9,10},{10,1... | collective-permute-start | bytes 1572872 | tf_op jit(solution)/shard_map/ppermute | solution.py:80
  210.2 10.7 %collective-permute-start.6 = (bf16[512,512]{1,0:T(8,128)(2,1)}, bf16[512,512]{1,0:T(8,128)(2,1)}, u32[]{:S(2)}, u32[]{:S(2)}) collective-permute-start(bf16[512,512]{1,0:T(8,128)(2,1)} %collective-permute-done.5), channel_id=1, source_target_pairs={{0,1},{1,2},{2,3},{3,4},{4,5},{5,6},{6,7},{7,0},{8,9},{9,10},{10,1... | collective-permute-start | bytes 1572872 | tf_op jit(solution)/shard_map/ppermute | solution.py:80
  210.2 21.9 %copy-start.15 = (bf16[512,512]{1,0:T(8,128)(2,1)S(1)}, bf16[512,512]{1,0:T(8,128)(2,1)}, u32[]{:S(2)}) copy-start(bf16[512,512]{1,0:T(8,128)(2,1)} %copy-done.14) | copy-start | bytes 1572868
  210.2 22.0 %copy-start.13 = (bf16[512,512]{1,0:T(8,128)(2,1)S(1)}, bf16[512,512]{1,0:T(8,128)(2,1)}, u32[]{:S(2)}) copy-start(bf16[512,512]{1,0:T(8,128)(2,1)} %copy-done.12) | copy-start | bytes 1572868
  210.2 22.0 %copy-start.11 = (bf16[512,512]{1,0:T(8,128)(2,1)S(1)}, bf16[512,512]{1,0:T(8,128)(2,1)}, u32[]{:S(2)}) copy-start(bf16[512,512]{1,0:T(8,128)(2,1)} %copy-done.10) | copy-start | bytes 1572868
  210.2 22.1 %copy-start.9 = (bf16[512,512]{1,0:T(8,128)(2,1)S(1)}, bf16[512,512]{1,0:T(8,128)(2,1)}, u32[]{:S(2)}) copy-start(bf16[512,512]{1,0:T(8,128)(2,1)} %copy-done.8) | copy-start | bytes 1572868
  210.2 22.1 %copy-start.7 = (bf16[512,512]{1,0:T(8,128)(2,1)S(1)}, bf16[512,512]{1,0:T(8,128)(2,1)}, u32[]{:S(2)}) copy-start(bf16[512,512]{1,0:T(8,128)(2,1)} %copy-done.6) | copy-start | bytes 1572868
  210.2 22.2 %copy-start.2 = (bf16[512,512]{1,0:T(8,128)(2,1)S(1)}, bf16[512,512]{1,0:T(8,128)(2,1)}, u32[]{:S(2)}) copy-start(bf16[512,512]{1,0:T(8,128)(2,1)} %copy-done.1) | copy-start | bytes 1572868
  210.2 25.5 %copy-start.17 = (bf16[4,128,512]{2,1,0:T(8,128)(2,1)S(1)}, bf16[4,128,512]{2,1,0:T(8,128)(2,1)}, u32[]{:S(2)}) copy-start(bf16[4,128,512]{2,1,0:T(8,128)(2,1)} %fusion.6) | copy-start | bytes 1572868
  232.5 3.3 copy-start.19
  246.1 30.1 %copy-start.3 = (bf16[512,512]{0,1:T(8,128)(2,1)}, bf16[512,512]{0,1:T(8,128)(2,1)S(1)}, u32[]{:S(2)}) copy-start(bf16[512,512]{0,1:T(8,128)(2,1)S(1)} %fusion.3) | copy-start | bytes 1572868
  246.1 30.1 %copy-start.16 = (bf16[512,512]{1,0:T(8,128)(2,1)S(1)}, bf16[512,512]{1,0:T(8,128)(2,1)}, u32[]{:S(2)}) copy-start(bf16[512,512]{1,0:T(8,128)(2,1)} %param.6) | copy-start | bytes 1572868
Sparse Core Ops, SparseCore 0:
  10.5 54.1 all-gather.3
  71.6 55.0 reduce-scatter.2
  240.3 88.3 reduce-scatter.4
